TPU v7x, 256 devices: a whole 4x4x8 slice. The times are simulated.
256 devices in a mesh: seq: 32 (over z, x), tp: 8 (over y, core).
Axes of the slice: x: 4, y: 4, z: 8, core: 2. Of those that a mesh axis runs over, the one named last changes fastest.
Arguments:
- grad_out: bfloat16 [8192, 4096], P('seq', 'tp'), may hold values from -6 to 6
- out_weight: bfloat16 [4096, 4096], P('tp'), may hold values from -0.09375 to 0.09375
- queries: bfloat16 [8192, 4096], P('seq', 'tp'), may hold values from -45 to 45
- keys: bfloat16 [8192, 4096], P('seq', 'tp'), may hold values from -4 to 4
- values: bfloat16 [8192, 4096], P('seq', 'tp'), may hold values from -6 to 6
- visible: int32 [64, 3], replicated, may hold values from 0 to 63, as said below
- live: int32 [64], replicated, may hold values from 1 to 3
Outputs:
- grad_queries: bfloat16 [8192, 4096], P('seq', 'tp')
- grad_keys: bfloat16 [8192, 4096], P('seq', 'tp')
- grad_values: bfloat16 [8192, 4096], P('seq', 'tp')
Inputs may be any that keep to these rules, and one draw needn't show every extreme that they name: `visible`: row a lists blocks that lie on other shards than a's (block b lies on shard b // 2); the rows of one shard never list a block twice, and list at most 1 block of any one other shard, a bound that some shard reaches.
All inputs are finite; a program needn't handle non-finite values.
Results may differ from a plain program's by a relative error of at most 0.014.
Values may be sent and summed in bfloat16 or wider, within the bound.
A program may use at most 128 MiB of HBM per device.

v0:
```python
import math

import jax
import jax.numpy as jnp
from jax import lax
from jax.sharding import PartitionSpec as P

D_HEAD = 128
BLK = 128
BLK_DEV = 2
NREM = 3


def project_part(out_weight, piece):
    return lax.dot_general(
        piece, out_weight, (((1,), (1,)), ((), ())), preferred_element_type=jnp.float32
    )


def attend_group(query_group, dout_group, key_far, value_far, seen_mask, key_near, value_near):
    scaling = 1.0 / math.sqrt(D_HEAD)
    near_scores = (
        jnp.einsum("aihd,jhd->ahij", query_group, key_near, preferred_element_type=jnp.float32)
        * scaling
    )
    far_scores = (
        jnp.einsum("aihd,ajhd->ahij", query_group, key_far, preferred_element_type=jnp.float32)
        * scaling
    )
    far_scores = jnp.where(seen_mask[:, None, None, :], far_scores, -1e30)
    highest = jnp.maximum(jnp.max(near_scores, axis=3), jnp.max(far_scores, axis=3))[..., None]
    near_exp = jnp.exp(near_scores - highest)
    far_exp = jnp.exp(far_scores - highest)
    totals = jnp.sum(near_exp, axis=3, keepdims=True) + jnp.sum(far_exp, axis=3, keepdims=True)
    near_probs = near_exp / totals
    far_probs = far_exp / totals
    near_grad = jnp.einsum(
        "aihd,jhd->ahij", dout_group, value_near, preferred_element_type=jnp.float32
    )
    far_grad = jnp.einsum(
        "aihd,ajhd->ahij", dout_group, value_far, preferred_element_type=jnp.float32
    )
    row_delta = jnp.sum(near_probs * near_grad, axis=3, keepdims=True) + jnp.sum(
        far_probs * far_grad, axis=3, keepdims=True
    )
    near_ds = (near_probs * (near_grad - row_delta) * scaling).astype(jnp.bfloat16)
    far_ds = (far_probs * (far_grad - row_delta) * scaling).astype(jnp.bfloat16)
    grad_query = jnp.einsum("ahij,jhd->aihd", near_ds, key_near, preferred_element_type=jnp.float32)
    grad_query = grad_query + jnp.einsum(
        "ahij,ajhd->aihd", far_ds, key_far, preferred_element_type=jnp.float32
    )
    log_totals = (highest + jnp.log(totals))[..., 0]
    return (
        near_probs,
        far_probs,
        near_ds,
        far_ds,
        grad_query.astype(jnp.bfloat16),
        log_totals,
        row_delta[..., 0],
    )


def shards(grad_out, out_weight, queries, keys, values, visible, live):
    shard_count = lax.axis_size("seq")
    myself = lax.axis_index("seq")
    row_count, feature_width = queries.shape
    head_count = feature_width // D_HEAD
    entries = BLK_DEV * NREM
    capacity = min(BLK_DEV, -(-entries // (shard_count - 1)))
    slot_count = shard_count * capacity
    dout = project_part(out_weight, lax.all_gather(grad_out, "tp", axis=1, tiled=True)).astype(
        jnp.bfloat16
    )
    owners = (visible // BLK_DEV).reshape(shard_count, entries)
    block_within = (visible % BLK_DEV).reshape(shard_count, entries)
    living = (jnp.arange(NREM, dtype=jnp.int32)[None, :] < live[:, None]).reshape(
        shard_count, entries
    )
    positions = jnp.arange(entries, dtype=jnp.int32)
    earlier = positions[None, :] < positions[:, None]
    matching = (owners[:, :, None] == owners[:, None, :]) & living[:, None, :] & earlier[None, :, :]
    ranking = jnp.sum(matching.astype(jnp.int32), axis=2)
    slot_ids = jnp.arange(capacity, dtype=jnp.int32)
    chosen = (living & (owners == myself))[:, None, :] & (
        ranking[:, None, :] == slot_ids[None, :, None]
    )
    filled = jnp.any(chosen, axis=2).reshape(slot_count)
    send_index = jnp.sum(jnp.where(chosen, block_within[:, None, :], 0), axis=2).reshape(slot_count)
    key_blocks = keys.reshape(BLK_DEV, BLK, feature_width)
    value_blocks = values.reshape(BLK_DEV, BLK, feature_width)
    keep_slot = filled[:, None, None]
    send_keys = jnp.where(
        keep_slot, jnp.take(key_blocks, send_index, axis=0), jnp.zeros((), keys.dtype)
    )
    send_values = jnp.where(
        keep_slot, jnp.take(value_blocks, send_index, axis=0), jnp.zeros((), values.dtype)
    )
    fetched_keys, fetched_values = (
        lax.all_to_all(
            send_keys.reshape(shard_count, capacity, BLK, feature_width),
            "seq",
            split_axis=0,
            concat_axis=0,
            tiled=True,
        ),
        lax.all_to_all(
            send_values.reshape(shard_count, capacity, BLK, feature_width),
            "seq",
            split_axis=0,
            concat_axis=0,
            tiled=True,
        ),
    )
    my_owners = lax.dynamic_index_in_dim(owners, myself, 0, keepdims=False)
    my_ranks = lax.dynamic_index_in_dim(ranking, myself, 0, keepdims=False)
    my_living = lax.dynamic_index_in_dim(living, myself, 0, keepdims=False)
    fetch_index = my_owners * capacity + my_ranks
    key_far = jnp.take(fetched_keys.reshape(slot_count, BLK, feature_width), fetch_index, axis=0)
    value_far = jnp.take(
        fetched_values.reshape(slot_count, BLK, feature_width), fetch_index, axis=0
    )
    placement = (
        (jnp.arange(slot_count, dtype=jnp.int32)[:, None] == fetch_index[None, :])
        & my_living[None, :]
    ).astype(jnp.bfloat16)
    collect = (
        (jnp.arange(BLK_DEV, dtype=jnp.int32)[:, None] == send_index[None, :]) & filled[None, :]
    ).astype(jnp.bfloat16)
    group_size = math.gcd(BLK_DEV, max(1, 512 // BLK))
    group_count = BLK_DEV // group_size

    def grouped(array_in):
        return array_in.reshape((group_count, group_size) + array_in.shape[1:])

    query_blocks = grouped(queries.reshape(BLK_DEV, BLK, head_count, D_HEAD))
    dout_blocks = grouped(dout.reshape(BLK_DEV, BLK, head_count, D_HEAD))
    far_key_blocks = grouped(key_far.reshape(BLK_DEV, NREM * BLK, head_count, D_HEAD))
    far_value_blocks = grouped(value_far.reshape(BLK_DEV, NREM * BLK, head_count, D_HEAD))
    seen_blocks = grouped(jnp.repeat(my_living.reshape(BLK_DEV, NREM), BLK, axis=1))
    key_near = keys.reshape(row_count, head_count, D_HEAD)
    value_near = values.reshape(row_count, head_count, D_HEAD)

    def one_group(carry, inputs):
        near_key_acc, near_value_acc = carry
        query_group, dout_group, key_group, value_group, mask_group = inputs
        near_probs, far_probs, near_ds, far_ds, grad_query, log_totals, row_delta = attend_group(
            query_group, dout_group, key_group, value_group, mask_group, key_near, value_near
        )
        near_key_acc = near_key_acc + jnp.einsum(
            "ahij,aihd->jhd", near_ds, query_group, preferred_element_type=jnp.float32
        )
        near_value_acc = near_value_acc + jnp.einsum(
            "ahij,aihd->jhd",
            near_probs.astype(jnp.bfloat16),
            dout_group,
            preferred_element_type=jnp.float32,
        )
        far_key_term = jnp.einsum(
            "ahij,aihd->ajhd", far_ds, query_group, preferred_element_type=jnp.float32
        ).astype(jnp.bfloat16)
        far_value_term = jnp.einsum(
            "ahij,aihd->ajhd",
            far_probs.astype(jnp.bfloat16),
            dout_group,
            preferred_element_type=jnp.float32,
        ).astype(jnp.bfloat16)
        extra = (far_key_term, far_value_term)
        return ((near_key_acc, near_value_acc), (grad_query, extra))

    start = (
        jnp.zeros((row_count, head_count, D_HEAD), jnp.float32),
        jnp.zeros((row_count, head_count, D_HEAD), jnp.float32),
    )
    (near_keys, near_values), (grad_query_all, extra_all) = lax.scan(
        one_group, start, (query_blocks, dout_blocks, far_key_blocks, far_value_blocks, seen_blocks)
    )
    grad_queries = grad_query_all.reshape(row_count, feature_width)
    far_key_terms = extra_all[0].reshape(entries, BLK * feature_width)
    far_value_terms = extra_all[1].reshape(entries, BLK * feature_width)
    returned_keys = jnp.dot(placement, far_key_terms, preferred_element_type=jnp.float32).astype(
        jnp.bfloat16
    )
    returned_values = jnp.dot(
        placement, far_value_terms, preferred_element_type=jnp.float32
    ).astype(jnp.bfloat16)
    back_keys, back_values = (
        lax.all_to_all(
            returned_keys.reshape(shard_count, capacity, BLK, feature_width),
            "seq",
            split_axis=0,
            concat_axis=0,
            tiled=True,
        ),
        lax.all_to_all(
            returned_values.reshape(shard_count, capacity, BLK, feature_width),
            "seq",
            split_axis=0,
            concat_axis=0,
            tiled=True,
        ),
    )
    far_key_sum = jnp.dot(
        collect,
        back_keys.reshape(slot_count, BLK * feature_width),
        preferred_element_type=jnp.float32,
    )
    far_value_sum = jnp.dot(
        collect,
        back_values.reshape(slot_count, BLK * feature_width),
        preferred_element_type=jnp.float32,
    )
    grad_keys = (
        near_keys.reshape(row_count, feature_width) + far_key_sum.reshape(row_count, feature_width)
    ).astype(jnp.bfloat16)
    grad_values = (
        near_values.reshape(row_count, feature_width)
        + far_value_sum.reshape(row_count, feature_width)
    ).astype(jnp.bfloat16)
    return (grad_queries, grad_keys, grad_values)


def solution(mesh):
    placed = (
        P("seq", "tp"),
        P("tp", None),
        P("seq", "tp"),
        P("seq", "tp"),
        P("seq", "tp"),
        P(),
        P(),
    )
    return jax.shard_map(
        shards,
        mesh=mesh,
        in_specs=placed,
        out_specs=(P("seq", "tp"), P("seq", "tp"), P("seq", "tp")),
        check_vma=False,
    )
```

profile of v0, /device:TPU:24, one launch (start us, length us, event | category | flops | bytes accessed | tf_op | source)
XLA Modules:
  0.0 461.8 jit_solution(17356788205946980283)
XLA Ops:
  10.7 2.8 gather_fusion
  13.5 2.7 gather_fusion.2
  16.3 5.3 %fusion.1 = (bf16[32,1,128,512]{3,2,1,0:T(8,128)(2,1)S(1)}, bf16[32,1,128,512]{3,2,1,0:T(8,128)(2,1)}) fusion(bf16[32,128,512]{2,1,0:T(8,128)(2,1)} %gather_fusion, pred[32]{0:T(512)(128)(4,1)S(1)} %compare_and_fusion.1, pred[32]{0:T(512)(128)(4,1)S(1)} %get-tuple-element.31, bf16[32,128,512]{2,1,0:T(8,128)(2,1)} %gather_fusion.2), kind=kLoop, calls=%fused_computation.9 | loop fusion | flops 8388608 | bytes 16777280 | tf_op jit(solution)/shard_map/reshape | solution.py:101
  21.6 106.7 %all_to_all.20 = bf16[32,1,128,512]{3,2,1,0:T(8,128)(2,1)} all-to-all(bf16[32,1,128,512]{3,2,1,0:T(8,128)(2,1)S(1)} %get-tuple-element.35), channel_id=1, replica_groups=mesh['seq'=32,'tp'=8] {'seq'}, dimensions={0} | all-to-all | bytes 8388608 | tf_op jit(solution)/shard_map/all_to_all | solution.py:100
  128.2 5.8 %all-to-all-start.1 = ((bf16[32,1,128,512]{3,2,1,0:T(8,128)(2,1)}), bf16[32,1,128,512]{3,2,1,0:T(8,128)(2,1)}, u32[]{:S(2)}, u32[]{:S(2)}) async-start(bf16[32,1,128,512]{3,2,1,0:T(8,128)(2,1)} %get-tuple-element.36), calls=%async_computation.1 | async-start | bytes 8388608 | tf_op jit(solution)/shard_map/all_to_all | solution.py:107
  136.1 28.0 %all-gather.2.cloned.1.call-done = bf16[256,4096]{1,0:T(8,128)(2,1)} async-done(((bf16[256,512]{1,0:T(8,128)(2,1)}), bf16[256,4096]{1,0:T(8,128)(2,1)}) %all-gather.2.cloned.1.call-update) | async-done | bytes 2097168 | tf_op jit(solution)/shard_map/all_gather | solution.py:72
  164.1 4.1 convolution_convert_fusion.4
  169.2 2.8 gather_fusion.1
  172.0 55.4 %all-to-all-done.1 = bf16[32,1,128,512]{3,2,1,0:T(8,128)(2,1)} async-done(((bf16[32,1,128,512]{3,2,1,0:T(8,128)(2,1)}), bf16[32,1,128,512]{3,2,1,0:T(8,128)(2,1)}, u32[]{:S(2)}, u32[]{:S(2)}) %all-to-all-start.1) | async-done | bytes 4194336 | tf_op jit(solution)/shard_map/all_to_all | solution.py:107
  227.4 2.8 gather_fusion.3
  230.2 1.4 broadcast_select_fusion.1
  231.5 2.4 squeeze.27
  234.0 1.6 bitcast_reduce_fusion
  236.7 1.4 fusion.7
  238.0 2.2 copy.328
  240.2 2.7 reshape.287
  242.9 2.4 convolution_convert_fusion
  245.3 3.5 copy.355
  248.8 7.1 %all-to-all-start.3 = ((bf16[32,1,128,512]{3,2,1,0:T(8,128)(2,1)}), bf16[32,1,128,512]{3,2,1,0:T(8,128)(2,1)}, u32[]{:S(2)}, u32[]{:S(2)}) async-start(bf16[32,1,128,512]{3,2,1,0:T(8,128)(2,1)} %bitcast.112), calls=%async_computation.3 | async-start | bytes 8388608 | tf_op jit(solution)/shard_map/all_to_all | solution.py:195
  257.9 2.5 squeeze.29
  260.4 2.4 multiply_reduce_fusion.1
  263.3 1.8 multiply_convert_fusion
  265.5 1.5 copy.321
  267.0 1.7 reshape.282
  268.7 1.2 convolution_convert_fusion.1
  269.9 3.5 copy.353
  273.4 75.3 %all-to-all-done.3 = bf16[32,1,128,512]{3,2,1,0:T(8,128)(2,1)} async-done(((bf16[32,1,128,512]{3,2,1,0:T(8,128)(2,1)}), bf16[32,1,128,512]{3,2,1,0:T(8,128)(2,1)}, u32[]{:S(2)}, u32[]{:S(2)}) %all-to-all-start.3) | async-done | bytes 4194336 | tf_op jit(solution)/shard_map/all_to_all | solution.py:195
  348.7 7.1 %all-to-all-start.2 = ((bf16[32,1,128,512]{3,2,1,0:T(8,128)(2,1)}), bf16[32,1,128,512]{3,2,1,0:T(8,128)(2,1)}, u32[]{:S(2)}, u32[]{:S(2)}) async-start(bf16[32,1,128,512]{3,2,1,0:T(8,128)(2,1)} %bitcast.111), calls=%async_computation.2 | async-start | bytes 8388608 | tf_op jit(solution)/shard_map/all_to_all | solution.py:188
  355.9 1.6 multiply_convert_fusion.1
  360.7 4.6 copy.356
  366.4 81.9 %all-to-all-done.2 = bf16[32,1,128,512]{3,2,1,0:T(8,128)(2,1)} async-done(((bf16[32,1,128,512]{3,2,1,0:T(8,128)(2,1)}), bf16[32,1,128,512]{3,2,1,0:T(8,128)(2,1)}, u32[]{:S(2)}, u32[]{:S(2)}) %all-to-all-start.2) | async-done | bytes 4194336 | tf_op jit(solution)/shard_map/all_to_all | solution.py:188
  448.3 4.6 copy.354
  (93 shorter events, 16.6 us)
Async XLA Ops:
  7.2 3.5 copy-start
  10.7 2.8 copy-start.1
  128.2 6.7 %copy-start.8 = (bf16[256,512]{1,0:T(8,128)(2,1)S(1)}, bf16[256,512]{1,0:T(8,128)(2,1)}, u32[]{:S(2)}) copy-start(bf16[256,512]{1,0:T(8,128)(2,1)} %param.13) | copy-start | bytes 786436
  128.2 99.1 %all-to-all-start.1 = ((bf16[32,1,128,512]{3,2,1,0:T(8,128)(2,1)}), bf16[32,1,128,512]{3,2,1,0:T(8,128)(2,1)}, u32[]{:S(2)}, u32[]{:S(2)}) async-start(bf16[32,1,128,512]{3,2,1,0:T(8,128)(2,1)} %get-tuple-element.36), calls=%async_computation.1 | async-start | bytes 8388608 | tf_op jit(solution)/shard_map/all_to_all | solution.py:107
  134.1 30.0 %all-gather.2.cloned.1.call-start = ((), (), s32[]{:S(2)}) async-start(), calls=%async_computation.4 | async-start | bytes 2359296 | tf_op jit(solution)/shard_map/all_gather | solution.py:72
  135.6 32.7 %copy-start.4 = (bf16[2,128,4,128]{1,3,0,2:T(8,128)(2,1)}, bf16[2,128,4,128]{1,3,0,2:T(8,128)(2,1)S(1)}, u32[]{:S(2)}) copy-start(bf16[2,128,4,128]{1,3,0,2:T(8,128)(2,1)S(1)} %copy.319) | copy-start | bytes 786436
  168.3 0.9 copy-start.6
  235.5 27.3 %copy-start.2 = (f32[2,4,384,128]{3,2,1,0:T(8,128)}, f32[2,4,384,128]{3,2,1,0:T(8,128)S(1)}, u32[]{:S(2)}) copy-start(f32[2,4,384,128]{3,2,1,0:T(8,128)S(1)} %get-tuple-element.53) | copy-start | bytes 4718596
  235.5 1.1 copy-start.11
  248.8 100.0 %all-to-all-start.3 = ((bf16[32,1,128,512]{3,2,1,0:T(8,128)(2,1)}), bf16[32,1,128,512]{3,2,1,0:T(8,128)(2,1)}, u32[]{:S(2)}, u32[]{:S(2)}) async-start(bf16[32,1,128,512]{3,2,1,0:T(8,128)(2,1)} %bitcast.112), calls=%async_computation.3 | async-start | bytes 8388608 | tf_op jit(solution)/shard_map/all_to_all | solution.py:195
  257.9 4.9 %copy-start.9 = (bf16[2,128,4,128]{1,3,0,2:T(8,128)(2,1)}, bf16[2,128,4,128]{1,3,0,2:T(8,128)(2,1)S(1)}, u32[]{:S(2)}) copy-start(bf16[2,128,4,128]{1,3,0,2:T(8,128)(2,1)S(1)} %copy.324) | copy-start | bytes 786436
  260.4 2.4 copy-start.7
  260.4 2.4 copy-start.12
  348.7 99.6 %all-to-all-start.2 = ((bf16[32,1,128,512]{3,2,1,0:T(8,128)(2,1)}), bf16[32,1,128,512]{3,2,1,0:T(8,128)(2,1)}, u32[]{:S(2)}, u32[]{:S(2)}) async-start(bf16[32,1,128,512]{3,2,1,0:T(8,128)(2,1)} %bitcast.111), calls=%async_computation.2 | async-start | bytes 8388608 | tf_op jit(solution)/shard_map/all_to_all | solution.py:188
  355.9 2.0 copy-start.3
  357.5 1.8 copy-start.10
  359.3 1.0 copy-start.5
Sparse Core Ops, SparseCore 0:
  136.7 27.3 all-gather.1
where the time goes:
time: 464 us; the launch traced here: 462 us
  waiting for transfers between devices  241 us (52%)
  blocking collectives  107 us (23%)
  local copies, waits for them, and re-layouts  48.9 us (11%)
  starting transfers between devices  20.1 us (4%)
  matrix products  16.9 us (4%)
  between operations  14.5 us (3%)
  other arithmetic  13.3 us (3%)
    all_to_all x1, blocking collectives, shards(): lax.all_to_all(send_keys.reshape(shard_count, capacity, BLK, feature_widt...  107 us
    all_to_all x1, waiting for transfers between devices, shards(): lax.all_to_all(returned_keys.reshape(shard_count, capacity, BLK, feature_...  81.9 us
    all_to_all x1, waiting for transfers between devices, shards(): lax.all_to_all(returned_values.reshape(shard_count, capacity, BLK, featur...  75.3 us
    all_to_all x1, waiting for transfers between devices, shards(): lax.all_to_all(send_values.reshape(shard_count, capacity, BLK, feature_wi...  55.4 us
    all_gather x1, waiting for transfers between devices, shards(): lax.all_gather(grad_out, 'tp', axis=1, tiled=True)  28 us
    unnamed x33, local copies, waits for them, and re-layouts  18.1 us
  transfers between devices with their start and end apart: 4, of which 4 were waited for; matrix products, arithmetic and copies ran while one was open for 8% of the time, Pallas kernels for 0%

commit v1 on v0

v1 whole, which is shorter than its diff:
```python
import functools
import math

import jax
import jax.numpy as jnp
from jax import lax
from jax.experimental import pallas as pl
from jax.experimental.pallas import tpu as pltpu
from jax.sharding import PartitionSpec as P

MESH = pl.DeviceIdType.MESH
BF16 = jnp.bfloat16
F32 = jnp.float32

D_HEAD = 128
BLK = 128
BLK_DEV = 2
NREM = 3
ENTRIES = BLK_DEV * NREM
NZ, NX = 8, 4
SHARDS = NZ * NX
NBLK = SHARDS * BLK_DEV
CHUNK = 32
HALF = CHUNK // 2
SCALE = 1.0 / math.sqrt(D_HEAD)

SERVED = (
    [(dz, dx, 0, CHUNK) for dz in (0, 1, NZ - 1) for dx in range(NX)]
    + [(2, dx, HALF, HALF) for dx in range(NX)]
    + [(NZ - 2, dx, 0, HALF) for dx in range(NX)]
)
SLOT = {(dz, dx): i for i, (dz, dx, _, _) in enumerate(SERVED)}
FULL_SLOTS = 16

P1K, P1V, P2K, P2V, R1V, R1K, R2V, R2K, GATHER = range(9)


def dot(a, b, contract):
    return lax.dot_general(a, b, ((contract[:1], contract[1:]), ((), ())), preferred_element_type=F32)


def kernel(
    tp_size,
    visible, live, inverse,
    g_hbm, w_hbm, q_hbm, k_hbm, v_hbm,
    dq_ref, dk_ref, dv_ref,
    g_v, w_v, q_v, k_v, v_v, g_all, do_v,
    hold_k, hold_v, pick_k, pick_v, far_k, far_v,
    back_v, back_k, got_v, got_k, sum_v, sum_k, fin_v, fin_k,
    near_p, far_p, near_dv, near_dk,
    send, recv, load,
):
    me = lax.axis_index("seq")
    tp = lax.axis_index("tp")
    z, x = lax.div(me, NX), lax.rem(me, NX)
    others = [(dz, dx) for dz in range(NZ) for dx in range(NX) if (dz, dx) != (0, 0)]

    def shard_at(dz, dx):
        return lax.rem(z + dz, NZ) * NX + lax.rem(x + dx, NX)

    barrier = pltpu.get_barrier_semaphore()
    for dz, dx in others:
        pl.semaphore_signal(barrier, inc=1, device_id=(shard_at(dz, dx), tp), device_id_type=MESH)
    for dt in range(1, tp_size):
        pl.semaphore_signal(barrier, inc=1, device_id=(me, lax.rem(tp + dt, tp_size)), device_id_type=MESH)
    loads = [
        pltpu.make_async_copy(src, dst, load.at[i])
        for i, (src, dst) in enumerate(((k_hbm, k_v), (g_hbm, g_v), (v_hbm, v_v), (q_hbm, q_v), (w_hbm, w_v)))
    ]
    for copy in loads:
        copy.start()
    loads[0].wait()
    loads[1].wait()
    loads[2].wait()
    pl.semaphore_wait(barrier, len(others) + tp_size - 1)

    def remote(src, dst, phase, device):
        pltpu.make_async_remote_copy(
            src_ref=src, dst_ref=dst, send_sem=send.at[phase], recv_sem=recv.at[phase],
            device_id=device, device_id_type=MESH,
        ).start()

    def local(src, dst, phase):
        pltpu.make_async_copy(src, dst, recv.at[phase]).start()

    def arrived(ref, phase):
        pltpu.make_async_copy(ref, ref, recv.at[phase]).wait()

    def sent(ref, phase):
        pltpu.make_async_copy(ref, ref, send.at[phase]).wait()

    def chunk_of(zz):
        return pl.multiple_of(lax.rem(zz, NX) * CHUNK, CHUNK)

    def lanes_of(head):
        return pl.ds(pl.multiple_of(head * D_HEAD, D_HEAD), D_HEAD)

    my_blocks = pl.ds(me * BLK_DEV, BLK_DEV)

    def spread(own, hold, phase):
        def part(dz, dx):
            return own.at[:, pl.ds(chunk_of(z + dz), CHUNK), lanes_of(lax.rem(x + dx, NX))]

        for dz, dx in others:
            remote(part(dz, dx), hold.at[my_blocks], phase, (shard_at(dz, dx), tp))
        local(part(0, 0), hold.at[my_blocks], phase)

    spread(k_v, hold_k, P1K)
    for dt in range(1, tp_size):
        remote(g_v, g_all.at[tp], GATHER, (me, lax.rem(tp + dt, tp_size)))
    local(g_v, g_all.at[tp], GATHER)
    spread(v_v, hold_v, P1V)

    loads[3].wait()

    def near_scores(head, _):
        lanes = lanes_of(head)
        keys = k_v[:, :, lanes].reshape(BLK_DEV * BLK, D_HEAD)
        near_p[head] = dot(keys, q_v[:, lanes], (1, 1)) * SCALE
        return 0

    lax.fori_loop(0, NX, near_scores, 0)

    def forward(hold, pick, far, phase):
        for i, (dz, dx, first, rows) in enumerate(SERVED):
            shard = shard_at(dz, dx)
            for e in range(ENTRIES):
                block = visible[shard * ENTRIES + e]
                pick[i, e, first : first + rows] = hold[block, first : first + rows]
        for i, (dz, dx, first, rows) in enumerate(SERVED):
            src = pick.at[i, :, pl.ds(first, rows)]
            dst = far.at[:, x, pl.ds(pl.multiple_of(chunk_of(z) + first, HALF), rows)]
            if i == 0:
                local(src, dst, phase)
            else:
                remote(src, dst, phase, (shard_at(dz, dx), tp))

    arrived(hold_k, P1K)
    forward(hold_k, pick_k, far_k, P2K)
    arrived(hold_v, P1V)
    forward(hold_v, pick_v, far_v, P2V)

    loads[4].wait()
    arrived(g_all, GATHER)
    width = g_v.shape[1]
    total = dot(g_all[0], w_v[:, :width], (1, 1))
    for t in range(1, tp_size):
        total += dot(g_all[t], w_v[:, t * width : (t + 1) * width], (1, 1))
    do_v[...] = total.astype(BF16)

    def return_far(back, got, phase, dx):
        head = lax.rem(x + dx, NX)
        for dz in (0, 1, NZ - 1, 2, NZ - 2):
            slot = SLOT[((NZ - dz) % NZ, (NX - dx) % NX)]
            _, _, first, rows = SERVED[slot]
            src = back.at[:, head, pl.ds(pl.multiple_of(chunk_of(z + dz) + first, HALF), rows)]
            dst = got.at[slot, pl.ds(0, ENTRIES), pl.ds(first, rows)]
            if slot == 0:
                local(src, dst, phase)
            else:
                remote(src, dst, phase, (shard_at(dz, dx), tp))

    arrived(far_k, P2K)
    for dx in range(NX):
        head = lax.rem(x + dx, NX)
        lanes = lanes_of(head)
        pieces = []
        for a in range(BLK_DEV):
            rows = slice(a * BLK, (a + 1) * BLK)
            near = near_p[head, :, rows]
            keys = far_k[a * NREM : (a + 1) * NREM, head].reshape(NREM * BLK, D_HEAD)
            far = dot(keys, q_v[rows, lanes], (1, 1)) * SCALE
            count = live[me * BLK_DEV + a]
            entry = lax.broadcasted_iota(jnp.int32, far.shape, 0) // BLK
            far = jnp.where(entry < count, far, -1e30)
            highest = jnp.maximum(jnp.max(near, axis=0, keepdims=True), jnp.max(far, axis=0, keepdims=True))
            near = jnp.exp(near - highest)
            far = jnp.exp(far - highest)
            scale = 1.0 / (jnp.sum(near, axis=0, keepdims=True) + jnp.sum(far, axis=0, keepdims=True))
            near = near * scale
            far = far * scale
            near_p[head, :, rows] = near
            far_p[head, a] = far
            far_dv = dot(far.astype(BF16), do_v[rows, lanes], (1, 0)).astype(BF16)
            back_v[a * NREM : (a + 1) * NREM, head] = far_dv.reshape(NREM, BLK, D_HEAD)
            pieces.append(near.astype(BF16))
        return_far(back_v, got_v, R1V, dx)
        near_dv[head] = dot(jnp.concatenate(pieces, axis=1), do_v[:, lanes], (1, 0))

    arrived(far_v, P2V)
    for dx in range(NX):
        head = lax.rem(x + dx, NX)
        lanes = lanes_of(head)
        values = v_v[:, :, lanes].reshape(BLK_DEV * BLK, D_HEAD)
        near_grad = dot(values, do_v[:, lanes], (1, 1))
        pieces, fars = [], []
        for a in range(BLK_DEV):
            rows = slice(a * BLK, (a + 1) * BLK)
            far_values = far_v[a * NREM : (a + 1) * NREM, head].reshape(NREM * BLK, D_HEAD)
            grad = dot(far_values, do_v[rows, lanes], (1, 1))
            near, far = near_p[head, :, rows], far_p[head, a]
            own = near_grad[:, rows]
            delta = jnp.sum(near * own, axis=0, keepdims=True) + jnp.sum(far * grad, axis=0, keepdims=True)
            near = (near * (own - delta) * SCALE).astype(BF16)
            far = (far * (grad - delta) * SCALE).astype(BF16)
            far_dk = dot(far, q_v[rows, lanes], (1, 0)).astype(BF16)
            back_k[a * NREM : (a + 1) * NREM, head] = far_dk.reshape(NREM, BLK, D_HEAD)
            pieces.append(near)
            fars.append(far)
        return_far(back_k, got_k, R1K, dx)
        near = jnp.concatenate(pieces, axis=1)
        near_dk[head] = dot(near, q_v[:, lanes], (1, 0))
        keys = k_v[:, :, lanes].reshape(BLK_DEV * BLK, D_HEAD)
        near_dq = dot(near, keys, (0, 0))
        for a in range(BLK_DEV):
            rows = slice(a * BLK, (a + 1) * BLK)
            keys = far_k[a * NREM : (a + 1) * NREM, head].reshape(NREM * BLK, D_HEAD)
            dq_ref[rows, lanes] = (near_dq[rows] + dot(fars[a], keys, (0, 0))).astype(BF16)

    served = [shard_at(dz, dx) * NBLK for dz, dx, _, _ in SERVED]
    zeros = jnp.zeros((CHUNK, D_HEAD), BF16)

    def collect(got, sums, fin, phase):
        def one_block(block, _):
            upper = jnp.zeros((HALF, D_HEAD), F32)
            lower = jnp.zeros((HALF, D_HEAD), F32)
            for i, (_, _, first, rows) in enumerate(SERVED):
                e = inverse[served[i] + block]
                if first == 0:
                    upper += got[i, e, :HALF].astype(F32)
                if first + rows == CHUNK:
                    lower += got[i, e, HALF:].astype(F32)
            sums[block, :HALF] = upper.astype(BF16)
            sums[block, HALF:] = lower.astype(BF16)
            return 0

        lax.fori_loop(0, NBLK, one_block, 0)
        dst = fin.at[lax.div(z, NX), x, :, pl.ds(chunk_of(z), CHUNK)]
        for dz, dx in others:
            shard = shard_at(dz, dx)
            remote(sums.at[pl.ds(shard * BLK_DEV, BLK_DEV)], dst, phase, (shard, tp))
        local(sums.at[my_blocks], dst, phase)

    counted = (pl.ds(0, FULL_SLOTS), pl.ds(0, ENTRIES))
    for i in range(len(SERVED)):
        got_v[i, ENTRIES] = zeros
        got_k[i, ENTRIES] = zeros
    arrived(got_v.at[counted], R1V)
    collect(got_v, sum_v, fin_v, R2V)
    arrived(got_k.at[counted], R1K)
    collect(got_k, sum_k, fin_k, R2K)

    def finish(near, fin, out):
        for head in range(NX):
            total = near[head]
            for copy in range(2):
                total += fin[copy, head].reshape(BLK_DEV * BLK, D_HEAD).astype(F32)
            out[:, head * D_HEAD : (head + 1) * D_HEAD] = total.astype(BF16)

    arrived(fin_v, R2V)
    finish(near_dv, fin_v, dv_ref)
    arrived(fin_k, R2K)
    finish(near_dk, fin_k, dk_ref)

    most = pl.ds(0, NBLK - BLK_DEV)
    sent(hold_k.at[most], P1K)
    sent(hold_v.at[most], P1V)
    sent(g_all.at[pl.ds(0, tp_size - 1)], GATHER)
    fewer = (pl.ds(0, FULL_SLOTS - 1), pl.ds(0, ENTRIES))
    sent(pick_k.at[fewer], P2K)
    sent(pick_v.at[fewer], P2V)
    sent(got_v.at[fewer], R1V)
    sent(got_k.at[fewer], R1K)
    sent(sum_v.at[most], R2V)
    sent(sum_k.at[most], R2K)


def shards(tp_size, grad_out, out_weight, queries, keys, values, visible, live):
    rows, features = queries.shape
    heads = features // D_HEAD
    listed = visible.reshape(SHARDS, ENTRIES).astype(jnp.int32)
    blocks = jnp.arange(NBLK, dtype=jnp.int32)
    entry = jnp.arange(ENTRIES, dtype=jnp.int32)
    hit = listed[:, :, None] == blocks[None, None, :]
    inverse = jnp.min(jnp.where(hit, entry[None, :, None], ENTRIES), axis=1).reshape(-1)
    smem = pl.BlockSpec(memory_space=pltpu.SMEM)
    anywhere = pl.BlockSpec(memory_space=pl.ANY)
    vmem = pl.BlockSpec(memory_space=pltpu.VMEM)
    out = jax.ShapeDtypeStruct((rows, features), BF16)
    tiles = pltpu.VMEM((NBLK, CHUNK, D_HEAD), BF16)
    picked = pltpu.VMEM((len(SERVED), ENTRIES, CHUNK, D_HEAD), BF16)
    far = pltpu.VMEM((ENTRIES, heads, BLK, D_HEAD), BF16)
    got = pltpu.VMEM((len(SERVED), ENTRIES + 1, CHUNK, D_HEAD), BF16)
    fin = pltpu.VMEM((2, heads, BLK_DEV, BLK, D_HEAD), BF16)
    near = pltpu.VMEM((heads, rows, D_HEAD), F32)
    split = (BLK_DEV, BLK, features)
    return pl.pallas_call(
        functools.partial(kernel, tp_size),
        out_shape=(out, out, out),
        in_specs=[smem, smem, smem] + [anywhere] * 5,
        out_specs=(vmem, vmem, vmem),
        scratch_shapes=[
            pltpu.VMEM(grad_out.shape, BF16),
            pltpu.VMEM(out_weight.shape, BF16),
            pltpu.VMEM(queries.shape, BF16),
            pltpu.VMEM(split, BF16),
            pltpu.VMEM(split, BF16),
            pltpu.VMEM((tp_size,) + grad_out.shape, BF16),
            pltpu.VMEM(queries.shape, BF16),
            tiles, tiles, picked, picked, far, far,
            far, far, got, got, tiles, tiles, fin, fin,
            pltpu.VMEM((heads, rows, rows), F32),
            pltpu.VMEM((heads, BLK_DEV, NREM * BLK, BLK), F32),
            near, near,
            pltpu.SemaphoreType.DMA((9,)),
            pltpu.SemaphoreType.DMA((9,)),
            pltpu.SemaphoreType.DMA((5,)),
        ],
        compiler_params=pltpu.CompilerParams(
            collective_id=0, has_side_effects=True, vmem_limit_bytes=56 * 2**20
        ),
    )(
        listed.reshape(-1), live, inverse,
        grad_out, out_weight, queries, keys.reshape(split), values.reshape(split),
    )


def solution(mesh):
    placed = (
        P("seq", "tp"),
        P("tp", None),
        P("seq", "tp"),
        P("seq", "tp"),
        P("seq", "tp"),
        P(),
        P(),
    )
    return jax.shard_map(
        functools.partial(shards, mesh.shape["tp"]),
        mesh=mesh,
        in_specs=placed,
        out_specs=(P("seq", "tp"), P("seq", "tp"), P("seq", "tp")),
        check_vma=False,
    )
```

time: 464 us -> 103 us (0.22)
  waiting for transfers between devices: 241 us -> 0 us
  blocking collectives: 107 us -> 0 us
  Pallas kernels: 0 us -> 94.4 us
  local copies, waits for them, and re-layouts: 48.9 us -> 7.3 us
  starting transfers between devices: 20.1 us -> 0 us
  matrix products: 16.9 us -> 0 us
  between operations: 14.5 us -> 0.65 us
  other arithmetic: 13.3 us -> 0.1 us
    all_to_all x3 -> x0, waiting for transfers between devices: 213 us -> none  [the longest x1 81.9 us: shards(): lax.all_to_all(returned_keys.reshape(shard_count, capacity, BLK, feature_...]
    all_to_all x1 -> x0, blocking collectives: 107 us -> none  [shards(): lax.all_to_all(send_keys.reshape(shard_count, capacity, BLK, feature_widt...]
    pallas_call x0 -> x1, Pallas kernels: none -> 94.4 us  [shards(): pl.pallas_call(functools.partial(kernel, tp_size), out_shape=(out, out, o...]
    all_gather x1 -> x0, waiting for transfers between devices: 28 us -> none  [shards(): lax.all_gather(grad_out, 'tp', axis=1, tiled=True)]
    all_to_all x3 -> x0, starting transfers between devices: 20.1 us -> none  [the longest x1 7.15 us: shards(): lax.all_to_all(returned_values.reshape(shard_count, capacity, BLK, featur...]
    dot_general x15 -> x0, matrix products: 16.9 us -> none  [the longest x1 4.1 us: project_part(): lax.dot_general(piece, out_weight, (((1,), (1,)), ((), ())), preferred_el...]
    unnamed x33 -> x4, local copies, waits for them, and re-layouts: 18.1 us -> 5.78 us
    gather x4 -> x0, local copies, waits for them, and re-layouts: 11.1 us -> none  [the longest x1 2.79 us: shards(): jnp.take(key_blocks, send_index, axis=0)]
  transfers between devices with their start and end apart: 4 -> 0, of which waited for: 4 -> 0; matrix products, arithmetic and copies ran while one was open for 8% -> 0% of each run, Pallas kernels for 0% -> 0%
where the time goes in v1:
time: 103 us; the launch traced here: 102 us
  Pallas kernels  94.4 us (92%)
  local copies, waits for them, and re-layouts  7.3 us (7%)
    pallas_call x1, Pallas kernels, shards(): pl.pallas_call(functools.partial(kernel, tp_size), out_shape=(out, out, o...  94.4 us
    unnamed x4, local copies, waits for them, and re-layouts  5.78 us

profile of v1, /device:TPU:24, one launch (start us, length us, event | category | flops | bytes accessed | tf_op | source)
XLA Modules:
  0.0 102.5 jit_solution(17578895895548732939)
XLA Ops:
  0.6 0.8 copy.12
  1.4 0.7 reshape_reshape.3.visible
  2.1 0.1 eq.15
  2.2 0.1 copy.14
  2.3 0.1 select_reduce_fusion
  2.4 0.7 reshape.16.inverse
  3.0 94.4 %shard_map.94 = (bf16[256,512]{1,0:T(8,128)(2,1)}, bf16[256,512]{1,0:T(8,128)(2,1)}, bf16[256,512]{1,0:T(8,128)(2,1)}) custom-call(s32[192]{0:T(256)} %reshape_reshape.3.visible, s32[64]{0:T(128)} %live.1, s32[2048]{0:T(1024)} %reshape.16.inverse, bf16[256,512]{1,0:T(8,128)(2,1)} %g_hbm.1, bf16[512,4096]{1,0:T(8,128)(2,1)} %w_hbm.1, bf16[256,512]{1,0:T(8,128)(2,1)} %q_hbm.1, ...), custom_call_target="tpu_custom_call" | custom-call | tf_op jit(solution)/shard_map/pallas_call | solution.py:297
  97.5 1.7 %copy.18 = bf16[256,512]{1,0:T(8,128)(2,1)} copy(bf16[256,512]{1,0:T(8,128)(2,1)} %get-tuple-element.6) | data formatting | bytes 524288
  99.1 1.7 %copy.19 = bf16[256,512]{1,0:T(8,128)(2,1)} copy(bf16[256,512]{1,0:T(8,128)(2,1)} %get-tuple-element.7) | data formatting | bytes 524288
  100.8 1.7 %copy.20 = bf16[256,512]{1,0:T(8,128)(2,1)} copy(bf16[256,512]{1,0:T(8,128)(2,1)} %get-tuple-element.8) | data formatting | bytes 524288

commit v2 on v1

--- a/solution.py
+++ b/solution.py
@@ -41,13 +41,13 @@
 
 def kernel(
     tp_size,
-    visible, live, inverse,
+    visible, live, listed,
     g_hbm, w_hbm, q_hbm, k_hbm, v_hbm,
     dq_ref, dk_ref, dv_ref,
     g_v, w_v, q_v, k_v, v_v, g_all, do_v,
     hold_k, hold_v, pick_k, pick_v, far_k, far_v,
     back_v, back_k, got_v, got_k, sum_v, sum_k, fin_v, fin_k,
-    near_p, far_p, near_dv, near_dk,
+    near_p, far_p, near_dv, near_dk, found, inverse,
     send, recv, load,
 ):
     me = lax.axis_index("seq")
@@ -69,6 +69,15 @@
     ]
     for copy in loads:
         copy.start()
+    shape = (NBLK, NBLK)
+    block = lax.broadcasted_iota(jnp.int32, shape, 0)
+    first_entry = lax.broadcasted_iota(jnp.int32, shape, 1) % BLK_DEV * NREM
+    place = jnp.full(shape, ENTRIES, jnp.int32)
+    for j in range(NREM):
+        place = jnp.where(listed[j : j + 1, :] == block, first_entry + j, place)
+    found[...] = place
+    table = pltpu.make_async_copy(found, inverse, load.at[5])
+    table.start()
     loads[0].wait()
     loads[1].wait()
     loads[2].wait()
@@ -125,7 +134,7 @@
         for i, (dz, dx, first, rows) in enumerate(SERVED):
             shard = shard_at(dz, dx)
             for e in range(ENTRIES):
-                block = visible[shard * ENTRIES + e]
+                block = visible[e % NREM, shard * BLK_DEV + e // NREM]
                 pick[i, e, first : first + rows] = hold[block, first : first + rows]
         for i, (dz, dx, first, rows) in enumerate(SERVED):
             src = pick.at[i, :, pl.ds(first, rows)]
@@ -217,7 +226,8 @@
             keys = far_k[a * NREM : (a + 1) * NREM, head].reshape(NREM * BLK, D_HEAD)
             dq_ref[rows, lanes] = (near_dq[rows] + dot(fars[a], keys, (0, 0))).astype(BF16)
 
-    served = [shard_at(dz, dx) * NBLK for dz, dx, _, _ in SERVED]
+    served = [shard_at(dz, dx) * BLK_DEV for dz, dx, _, _ in SERVED]
+    table.wait()
     zeros = jnp.zeros((CHUNK, D_HEAD), BF16)
 
     def collect(got, sums, fin, phase):
@@ -225,7 +235,7 @@
             upper = jnp.zeros((HALF, D_HEAD), F32)
             lower = jnp.zeros((HALF, D_HEAD), F32)
             for i, (_, _, first, rows) in enumerate(SERVED):
-                e = inverse[served[i] + block]
+                e = jnp.minimum(inverse[block, served[i]], inverse[block, served[i] + 1])
                 if first == 0:
                     upper += got[i, e, :HALF].astype(F32)
                 if first + rows == CHUNK:
@@ -275,16 +285,25 @@
     sent(sum_k.at[most], R2K)
 
 
+def write_out(a_ref, b_ref, c_ref, a_out, b_out, c_out, held, taken, put):
+    pairs = ((a_ref, a_out), (b_ref, b_out), (c_ref, c_out))
+    takes = [pltpu.make_async_copy(src, held.at[i], taken.at[i]) for i, (src, _) in enumerate(pairs)]
+    puts = [pltpu.make_async_copy(held.at[i], dst, put.at[i]) for i, (_, dst) in enumerate(pairs)]
+    for copy in takes:
+        copy.start()
+    for take, copy in zip(takes, puts):
+        take.wait()
+        copy.start()
+    for copy in puts:
+        copy.wait()
+
+
 def shards(tp_size, grad_out, out_weight, queries, keys, values, visible, live):
     rows, features = queries.shape
     heads = features // D_HEAD
-    listed = visible.reshape(SHARDS, ENTRIES).astype(jnp.int32)
-    blocks = jnp.arange(NBLK, dtype=jnp.int32)
-    entry = jnp.arange(ENTRIES, dtype=jnp.int32)
-    hit = listed[:, :, None] == blocks[None, None, :]
-    inverse = jnp.min(jnp.where(hit, entry[None, :, None], ENTRIES), axis=1).reshape(-1)
+    listed = visible.astype(jnp.int32).T
     smem = pl.BlockSpec(memory_space=pltpu.SMEM)
-    anywhere = pl.BlockSpec(memory_space=pl.ANY)
+    anywhere = pl.BlockSpec(memory_space=pltpu.HBM)
     vmem = pl.BlockSpec(memory_space=pltpu.VMEM)
     out = jax.ShapeDtypeStruct((rows, features), BF16)
     tiles = pltpu.VMEM((NBLK, CHUNK, D_HEAD), BF16)
@@ -294,10 +313,10 @@
     fin = pltpu.VMEM((2, heads, BLK_DEV, BLK, D_HEAD), BF16)
     near = pltpu.VMEM((heads, rows, D_HEAD), F32)
     split = (BLK_DEV, BLK, features)
-    return pl.pallas_call(
+    outs = pl.pallas_call(
         functools.partial(kernel, tp_size),
         out_shape=(out, out, out),
-        in_specs=[smem, smem, smem] + [anywhere] * 5,
+        in_specs=[smem, smem, vmem] + [anywhere] * 5,
         out_specs=(vmem, vmem, vmem),
         scratch_shapes=[
             pltpu.VMEM(grad_out.shape, BF16),
@@ -312,17 +331,30 @@
             pltpu.VMEM((heads, rows, rows), F32),
             pltpu.VMEM((heads, BLK_DEV, NREM * BLK, BLK), F32),
             near, near,
+            pltpu.VMEM((NBLK, NBLK), jnp.int32),
+            pltpu.SMEM((NBLK, NBLK), jnp.int32),
             pltpu.SemaphoreType.DMA((9,)),
             pltpu.SemaphoreType.DMA((9,)),
-            pltpu.SemaphoreType.DMA((5,)),
+            pltpu.SemaphoreType.DMA((6,)),
         ],
         compiler_params=pltpu.CompilerParams(
             collective_id=0, has_side_effects=True, vmem_limit_bytes=56 * 2**20
         ),
     )(
-        listed.reshape(-1), live, inverse,
+        listed, live, listed,
         grad_out, out_weight, queries, keys.reshape(split), values.reshape(split),
     )
+    return pl.pallas_call(
+        write_out,
+        out_shape=(out, out, out),
+        in_specs=[anywhere] * 3,
+        out_specs=(anywhere,) * 3,
+        scratch_shapes=[
+            pltpu.VMEM((3, rows, features), BF16),
+            pltpu.SemaphoreType.DMA((3,)),
+            pltpu.SemaphoreType.DMA((3,)),
+        ],
+    )(*outs)
 
 
 def solution(mesh):

time: 103 us -> 97.1 us (0.943)
  local copies, waits for them, and re-layouts: 7.3 us -> 0 us
  Pallas kernels: 94.4 us -> 96.4 us
    unnamed x4 -> x0, local copies, waits for them, and re-layouts: 5.78 us -> none
    pallas_call x0 -> x1, Pallas kernels: none -> 1.88 us  [shards(): pl.pallas_call(write_out, out_shape=(out, out, out), in_specs=[anywhere]...]
where the time goes in v2:
time: 97.1 us; the launch traced here: 97 us
  Pallas kernels  96.4 us (99%)
    pallas_call x1, Pallas kernels, shards(): pl.pallas_call(functools.partial(kernel, tp_size), out_shape=(out, out, o...  94.5 us

profile of v2, /device:TPU:24, one launch (start us, length us, event | category | flops | bytes accessed | tf_op | source)
XLA Modules:
  0.0 97.0 jit_solution(15902553051011015354)
XLA Ops:
  0.6 94.5 %shard_map.94 = (bf16[256,512]{1,0:T(8,128)(2,1)}, bf16[256,512]{1,0:T(8,128)(2,1)}, bf16[256,512]{1,0:T(8,128)(2,1)}) custom-call(s32[3,64]{1,0:T(4,128)} %bitcast.5, s32[64]{0:T(128)} %live.1, s32[3,64]{1,0:T(4,128)} %bitcast.6, bf16[256,512]{1,0:T(8,128)(2,1)} %g_hbm.1, bf16[512,4096]{1,0:T(8,128)(2,1)} %w_hbm.1, bf16[256,512]{1,0:T(8,128)(2,1)} %q_hbm.1, ...), custom_call_target="tpu_custom_call" | custom-call | tf_op jit(solution)/shard_map/pallas_call | solution.py:316
  95.1 1.9 %shard_map.95 = (bf16[256,512]{1,0:T(8,128)(2,1)}, bf16[256,512]{1,0:T(8,128)(2,1)}, bf16[256,512]{1,0:T(8,128)(2,1)}) custom-call(bf16[256,512]{1,0:T(8,128)(2,1)} %get-tuple-element.6.a_ref, bf16[256,512]{1,0:T(8,128)(2,1)} %get-tuple-element.7.b_ref, bf16[256,512]{1,0:T(8,128)(2,1)} %get-tuple-element.8.c_ref), custom_call_target="tpu_custom_call" | custom-call | tf_op jit(solution)/shard_map/pallas_call | solution.py:347

commit v3 on v2

--- a/solution.py
+++ b/solution.py
@@ -39,16 +39,24 @@
     return lax.dot_general(a, b, ((contract[:1], contract[1:]), ((), ())), preferred_element_type=F32)
 
 
+def add_terms(near, fin, out):
+    for head in range(NX):
+        total = near[head]
+        for copy in range(2):
+            total += fin[copy, head].reshape(BLK_DEV * BLK, D_HEAD).astype(F32)
+        out[:, head * D_HEAD : (head + 1) * D_HEAD] = total.astype(BF16)
+
+
 def kernel(
     tp_size,
     visible, live, listed,
     g_hbm, w_hbm, q_hbm, k_hbm, v_hbm,
-    dq_ref, dk_ref, dv_ref,
+    dq_hbm, dv_hbm, near_dk_hbm, fin_k,
     g_v, w_v, q_v, k_v, v_v, g_all, do_v,
     hold_k, hold_v, pick_k, pick_v, far_k, far_v,
-    back_v, back_k, got_v, got_k, sum_v, sum_k, fin_v, fin_k,
-    near_p, far_p, near_dv, near_dk, found, inverse,
-    send, recv, load,
+    back_v, back_k, got_v, got_k, sum_v, sum_k, fin_v,
+    dq_ref, dv_ref, near_p, far_p, near_dv, near_dk, found, inverse,
+    send, recv, load, store,
 ):
     me = lax.axis_index("seq")
     tp = lax.axis_index("tp")
@@ -226,6 +234,13 @@
             keys = far_k[a * NREM : (a + 1) * NREM, head].reshape(NREM * BLK, D_HEAD)
             dq_ref[rows, lanes] = (near_dq[rows] + dot(fars[a], keys, (0, 0))).astype(BF16)
 
+    stores = [
+        pltpu.make_async_copy(src, dst, store.at[i])
+        for i, (src, dst) in enumerate(((dq_ref, dq_hbm), (near_dk, near_dk_hbm), (dv_ref, dv_hbm)))
+    ]
+    stores[0].start()
+    stores[1].start()
+
     served = [shard_at(dz, dx) * BLK_DEV for dz, dx, _, _ in SERVED]
     table.wait()
     zeros = jnp.zeros((CHUNK, D_HEAD), BF16)
@@ -260,17 +275,11 @@
     arrived(got_k.at[counted], R1K)
     collect(got_k, sum_k, fin_k, R2K)
 
-    def finish(near, fin, out):
-        for head in range(NX):
-            total = near[head]
-            for copy in range(2):
-                total += fin[copy, head].reshape(BLK_DEV * BLK, D_HEAD).astype(F32)
-            out[:, head * D_HEAD : (head + 1) * D_HEAD] = total.astype(BF16)
-
     arrived(fin_v, R2V)
-    finish(near_dv, fin_v, dv_ref)
-    arrived(fin_k, R2K)
-    finish(near_dk, fin_k, dk_ref)
+    add_terms(near_dv, fin_v, dv_ref)
+    stores[2].start()
+    for copy in stores:
+        copy.wait()
 
     most = pl.ds(0, NBLK - BLK_DEV)
     sent(hold_k.at[most], P1K)
@@ -283,17 +292,24 @@
     sent(got_k.at[fewer], R1K)
     sent(sum_v.at[most], R2V)
     sent(sum_k.at[most], R2K)
-
-
-def write_out(a_ref, b_ref, c_ref, a_out, b_out, c_out, held, taken, put):
-    pairs = ((a_ref, a_out), (b_ref, b_out), (c_ref, c_out))
-    takes = [pltpu.make_async_copy(src, held.at[i], taken.at[i]) for i, (src, _) in enumerate(pairs)]
-    puts = [pltpu.make_async_copy(held.at[i], dst, put.at[i]) for i, (_, dst) in enumerate(pairs)]
+    arrived(fin_k, R2K)
+
+
+def write_out(dq, dv, near_dk, fin_k, dq_out, dk_out, dv_out, dq_v, dv_v, near_v, fin_v, dk_v, taken, put):
+    sources = ((near_dk, near_v), (fin_k, fin_v), (dq, dq_v), (dv, dv_v))
+    takes = [pltpu.make_async_copy(src, dst, taken.at[i]) for i, (src, dst) in enumerate(sources)]
+    results = ((dq_v, dq_out), (dv_v, dv_out), (dk_v, dk_out))
+    puts = [pltpu.make_async_copy(src, dst, put.at[i]) for i, (src, dst) in enumerate(results)]
     for copy in takes:
         copy.start()
-    for take, copy in zip(takes, puts):
-        take.wait()
-        copy.start()
+    takes[2].wait()
+    puts[0].start()
+    takes[3].wait()
+    puts[1].start()
+    takes[0].wait()
+    takes[1].wait()
+    add_terms(near_v, fin_v, dk_v)
+    puts[2].start()
     for copy in puts:
         copy.wait()
 
@@ -313,11 +329,13 @@
     fin = pltpu.VMEM((2, heads, BLK_DEV, BLK, D_HEAD), BF16)
     near = pltpu.VMEM((heads, rows, D_HEAD), F32)
     split = (BLK_DEV, BLK, features)
+    near_out = jax.ShapeDtypeStruct((heads, rows, D_HEAD), F32)
+    fin_out = jax.ShapeDtypeStruct((2, heads, BLK_DEV, BLK, D_HEAD), BF16)
     outs = pl.pallas_call(
         functools.partial(kernel, tp_size),
-        out_shape=(out, out, out),
+        out_shape=(out, out, near_out, fin_out),
         in_specs=[smem, smem, vmem] + [anywhere] * 5,
-        out_specs=(vmem, vmem, vmem),
+        out_specs=(anywhere,) * 4,
         scratch_shapes=[
             pltpu.VMEM(grad_out.shape, BF16),
             pltpu.VMEM(out_weight.shape, BF16),
@@ -327,7 +345,9 @@
             pltpu.VMEM((tp_size,) + grad_out.shape, BF16),
             pltpu.VMEM(queries.shape, BF16),
             tiles, tiles, picked, picked, far, far,
-            far, far, got, got, tiles, tiles, fin, fin,
+            far, far, got, got, tiles, tiles, fin,
+            pltpu.VMEM(queries.shape, BF16),
+            pltpu.VMEM(queries.shape, BF16),
             pltpu.VMEM((heads, rows, rows), F32),
             pltpu.VMEM((heads, BLK_DEV, NREM * BLK, BLK), F32),
             near, near,
@@ -336,6 +356,7 @@
             pltpu.SemaphoreType.DMA((9,)),
             pltpu.SemaphoreType.DMA((9,)),
             pltpu.SemaphoreType.DMA((6,)),
+            pltpu.SemaphoreType.DMA((3,)),
         ],
         compiler_params=pltpu.CompilerParams(
             collective_id=0, has_side_effects=True, vmem_limit_bytes=56 * 2**20
@@ -347,11 +368,14 @@
     return pl.pallas_call(
         write_out,
         out_shape=(out, out, out),
-        in_specs=[anywhere] * 3,
+        in_specs=[anywhere] * 4,
         out_specs=(anywhere,) * 3,
         scratch_shapes=[
-            pltpu.VMEM((3, rows, features), BF16),
-            pltpu.SemaphoreType.DMA((3,)),
+            pltpu.VMEM(queries.shape, BF16),
+            pltpu.VMEM(queries.shape, BF16),
+            near, fin,
+            pltpu.VMEM(queries.shape, BF16),
+            pltpu.SemaphoreType.DMA((4,)),
             pltpu.SemaphoreType.DMA((3,)),
         ],
     )(*outs)

time: 97.1 us -> 96.6 us (level)
  no operation moved by 1% of the time
where the time goes in v3:
time: 96.6 us; the launch traced here: 96.5 us
  Pallas kernels  95.8 us (99%)
    pallas_call x1, Pallas kernels, shards(): pl.pallas_call(functools.partial(kernel, tp_size), out_shape=(out, out, n...  93.6 us
    pallas_call x1, Pallas kernels, shards(): pl.pallas_call(write_out, out_shape=(out, out, out), in_specs=[anywhere]...  2.2 us

profile of v3, /device:TPU:24, one launch (start us, length us, event | category | flops | bytes accessed | tf_op | source)
XLA Modules:
  0.0 96.5 jit_solution(2861025284769225251)
XLA Ops:
  0.6 93.6 %shard_map.94 = (bf16[256,512]{1,0:T(8,128)(2,1)}, bf16[256,512]{1,0:T(8,128)(2,1)}, f32[4,256,128]{2,1,0:T(8,128)}, bf16[2,4,2,128,128]{4,3,2,1,0:T(8,128)(2,1)}) custom-call(s32[3,64]{1,0:T(4,128)} %bitcast.5, s32[64]{0:T(128)} %live.1, s32[3,64]{1,0:T(4,128)} %bitcast.6, bf16[256,512]{1,0:T(8,128)(2,1)} %g_hbm.1, bf16[512,4096]{1,0:T(8,128)(2,1)} %w_hbm.1, ...), custom_call_target="tpu_custom_call" | custom-call | tf_op jit(solution)/shard_map/pallas_call | solution.py:334
  94.3 2.2 %shard_map.95 = (bf16[256,512]{1,0:T(8,128)(2,1)}, bf16[256,512]{1,0:T(8,128)(2,1)}, bf16[256,512]{1,0:T(8,128)(2,1)}) custom-call(bf16[256,512]{1,0:T(8,128)(2,1)} %get-tuple-element.7.dq, bf16[256,512]{1,0:T(8,128)(2,1)} %get-tuple-element.8.dv, f32[4,256,128]{2,1,0:T(8,128)} %get-tuple-element.9.near_dk, bf16[2,4,2,128,128]{4,3,2,1,0:T(8,128)(2,1)} %get-tuple-element.10.fin_k), custom_call_target="tpu_custom_call" | custom-call | tf_op jit(solution)/shard_map/pallas_call | solution.py:368

commit v4 on v3

--- a/solution.py
+++ b/solution.py
@@ -39,12 +39,11 @@
     return lax.dot_general(a, b, ((contract[:1], contract[1:]), ((), ())), preferred_element_type=F32)
 
 
-def add_terms(near, fin, out):
-    for head in range(NX):
-        total = near[head]
-        for copy in range(2):
-            total += fin[copy, head].reshape(BLK_DEV * BLK, D_HEAD).astype(F32)
-        out[:, head * D_HEAD : (head + 1) * D_HEAD] = total.astype(BF16)
+def add_terms(near, fin, out, head):
+    total = near[head]
+    for copy in range(2):
+        total += fin[copy, head].reshape(BLK_DEV * BLK, D_HEAD).astype(F32)
+    out[:, head * D_HEAD : (head + 1) * D_HEAD] = total.astype(BF16)
 
 
 def kernel(
@@ -56,7 +55,7 @@
     hold_k, hold_v, pick_k, pick_v, far_k, far_v,
     back_v, back_k, got_v, got_k, sum_v, sum_k, fin_v,
     dq_ref, dv_ref, near_p, far_p, near_dv, near_dk, found, inverse,
-    send, recv, load, store,
+    send, recv, load, store, upward, downward,
 ):
     me = lax.axis_index("seq")
     tp = lax.axis_index("tp")
@@ -67,7 +66,8 @@
         return lax.rem(z + dz, NZ) * NX + lax.rem(x + dx, NX)
 
     barrier = pltpu.get_barrier_semaphore()
-    for dz, dx in others:
+    greeted = [(1, 0), (NZ - 1, 0)] + [(0, dx) for dx in range(1, NX)]
+    for dz, dx in greeted:
         pl.semaphore_signal(barrier, inc=1, device_id=(shard_at(dz, dx), tp), device_id_type=MESH)
     for dt in range(1, tp_size):
         pl.semaphore_signal(barrier, inc=1, device_id=(me, lax.rem(tp + dt, tp_size)), device_id_type=MESH)
@@ -89,7 +89,7 @@
     loads[0].wait()
     loads[1].wait()
     loads[2].wait()
-    pl.semaphore_wait(barrier, len(others) + tp_size - 1)
+    pl.semaphore_wait(barrier, len(greeted) + tp_size - 1)
 
     def remote(src, dst, phase, device):
         pltpu.make_async_remote_copy(
@@ -114,19 +114,40 @@
 
     my_blocks = pl.ds(me * BLK_DEV, BLK_DEV)
 
-    def spread(own, hold, phase):
-        def part(dz, dx):
-            return own.at[:, pl.ds(chunk_of(z + dz), CHUNK), lanes_of(lax.rem(x + dx, NX))]
-
-        for dz, dx in others:
-            remote(part(dz, dx), hold.at[my_blocks], phase, (shard_at(dz, dx), tp))
-        local(part(0, 0), hold.at[my_blocks], phase)
-
-    spread(k_v, hold_k, P1K)
+    def spread(own, hold, phase, dz):
+        for dx in range(NX):
+            src = own.at[:, pl.ds(chunk_of(z + dz), CHUNK), lanes_of(lax.rem(x + dx, NX))]
+            if (dz, dx) == (0, 0):
+                local(src, hold.at[my_blocks], phase)
+            else:
+                remote(src, hold.at[my_blocks], phase, (shard_at(dz, dx), tp))
+
+    def tell(semaphore, dz):
+        pl.semaphore_signal(semaphore, inc=1, device_id=(shard_at(dz, 0), tp), device_id_type=MESH)
+
+    tell(upward, NZ - 1)
+    tell(downward, 1)
+    spread(k_v, hold_k, P1K, 0)
+    half = NZ // 2
+    for step in range(1, half + 1):
+        pl.semaphore_wait(upward, 1)
+        if step < half:
+            tell(upward, NZ - 1)
+        spread(k_v, hold_k, P1K, step)
+        if step < half:
+            pl.semaphore_wait(downward, 1)
+            if step < half - 1:
+                tell(downward, 1)
+            spread(k_v, hold_k, P1K, NZ - step)
+            if step == 2:
+                spread(v_v, hold_v, P1V, 0)
+                spread(v_v, hold_v, P1V, 1)
+                spread(v_v, hold_v, P1V, NZ - 1)
     for dt in range(1, tp_size):
         remote(g_v, g_all.at[tp], GATHER, (me, lax.rem(tp + dt, tp_size)))
     local(g_v, g_all.at[tp], GATHER)
-    spread(v_v, hold_v, P1V)
+    for dz in range(2, NZ - 1):
+        spread(v_v, hold_v, P1V, dz)
 
     loads[3].wait()
 
@@ -276,7 +297,8 @@
     collect(got_k, sum_k, fin_k, R2K)
 
     arrived(fin_v, R2V)
-    add_terms(near_dv, fin_v, dv_ref)
+    for head in range(NX):
+        add_terms(near_dv, fin_v, dv_ref, head)
     stores[2].start()
     for copy in stores:
         copy.wait()
@@ -296,20 +318,29 @@
 
 
 def write_out(dq, dv, near_dk, fin_k, dq_out, dk_out, dv_out, dq_v, dv_v, near_v, fin_v, dk_v, taken, put):
-    sources = ((near_dk, near_v), (fin_k, fin_v), (dq, dq_v), (dv, dv_v))
-    takes = [pltpu.make_async_copy(src, dst, taken.at[i]) for i, (src, dst) in enumerate(sources)]
-    results = ((dq_v, dq_out), (dv_v, dv_out), (dk_v, dk_out))
-    puts = [pltpu.make_async_copy(src, dst, put.at[i]) for i, (src, dst) in enumerate(results)]
-    for copy in takes:
-        copy.start()
-    takes[2].wait()
-    puts[0].start()
-    takes[3].wait()
-    puts[1].start()
-    takes[0].wait()
-    takes[1].wait()
-    add_terms(near_v, fin_v, dk_v)
-    puts[2].start()
+    heads = near_dk.shape[0]
+    takes, puts = [], []
+    for head in range(heads):
+        lanes = pl.ds(head * D_HEAD, D_HEAD)
+        takes.append((
+            pltpu.make_async_copy(fin_k.at[:, head], fin_v.at[:, head], taken.at[2 * head]),
+            pltpu.make_async_copy(near_dk.at[head], near_v.at[head], taken.at[2 * head + 1]),
+        ))
+        puts.append(pltpu.make_async_copy(dk_v.at[:, lanes], dk_out.at[:, lanes], put.at[head]))
+    whole = ((dq, dq_v, dq_out), (dv, dv_v, dv_out))
+    for i, (src, held, dst) in enumerate(whole):
+        takes.append((pltpu.make_async_copy(src, held, taken.at[2 * heads + i]),))
+        puts.append(pltpu.make_async_copy(held, dst, put.at[heads + i]))
+    order = [heads, heads + 1] + list(range(heads))
+    for i in order:
+        for copy in takes[i]:
+            copy.start()
+    for i in order:
+        for copy in takes[i]:
+            copy.wait()
+        if i < heads:
+            add_terms(near_v, fin_v, dk_v, i)
+        puts[i].start()
     for copy in puts:
         copy.wait()
 
@@ -357,6 +388,8 @@
             pltpu.SemaphoreType.DMA((9,)),
             pltpu.SemaphoreType.DMA((6,)),
             pltpu.SemaphoreType.DMA((3,)),
+            pltpu.SemaphoreType.REGULAR,
+            pltpu.SemaphoreType.REGULAR,
         ],
         compiler_params=pltpu.CompilerParams(
             collective_id=0, has_side_effects=True, vmem_limit_bytes=56 * 2**20
@@ -375,8 +408,8 @@
             pltpu.VMEM(queries.shape, BF16),
             near, fin,
             pltpu.VMEM(queries.shape, BF16),
-            pltpu.SemaphoreType.DMA((4,)),
-            pltpu.SemaphoreType.DMA((3,)),
+            pltpu.SemaphoreType.DMA((2 * heads + 2,)),
+            pltpu.SemaphoreType.DMA((heads + 2,)),
         ],
     )(*outs)
 

time: 96.6 us -> 96.1 us (level)
  the two profiles are of different devices: /device:TPU:24 before, /device:TPU:64 now
where the time goes in v4:
time: 96.1 us; the launch traced here: 96 us
  Pallas kernels  95.4 us (99%)
    pallas_call x1, Pallas kernels, shards(): pl.pallas_call(functools.partial(kernel, tp_size), out_shape=(out, out, n...  93.2 us
    pallas_call x1, Pallas kernels, shards(): pl.pallas_call(write_out, out_shape=(out, out, out), in_specs=[anywhere]...  2.13 us

profile of v4, /device:TPU:64, one launch (start us, length us, event | category | flops | bytes accessed | tf_op | source)
XLA Modules:
  0.0 96.0 jit_solution(13834204843887344998)
XLA Ops:
  0.6 93.2 %shard_map.94 = (bf16[256,512]{1,0:T(8,128)(2,1)}, bf16[256,512]{1,0:T(8,128)(2,1)}, f32[4,256,128]{2,1,0:T(8,128)}, bf16[2,4,2,128,128]{4,3,2,1,0:T(8,128)(2,1)}) custom-call(s32[3,64]{1,0:T(4,128)} %bitcast.5, s32[64]{0:T(128)} %live.1, s32[3,64]{1,0:T(4,128)} %bitcast.6, bf16[256,512]{1,0:T(8,128)(2,1)} %g_hbm.1, bf16[512,4096]{1,0:T(8,128)(2,1)} %w_hbm.1, ...), custom_call_target="tpu_custom_call" | custom-call | tf_op jit(solution)/shard_map/pallas_call | solution.py:365
  93.9 2.1 %shard_map.95 = (bf16[256,512]{1,0:T(8,128)(2,1)}, bf16[256,512]{1,0:T(8,128)(2,1)}, bf16[256,512]{1,0:T(8,128)(2,1)}) custom-call(bf16[256,512]{1,0:T(8,128)(2,1)} %get-tuple-element.7.dq, bf16[256,512]{1,0:T(8,128)(2,1)} %get-tuple-element.8.dv, f32[4,256,128]{2,1,0:T(8,128)} %get-tuple-element.9.near_dk, bf16[2,4,2,128,128]{4,3,2,1,0:T(8,128)(2,1)} %get-tuple-element.10.fin_k), custom_call_target="tpu_custom_call" | custom-call | tf_op jit(solution)/shard_map/pallas_call | solution.py:401

commit v5 on v4

--- a/solution.py
+++ b/solution.py
@@ -141,12 +141,13 @@
             spread(k_v, hold_k, P1K, NZ - step)
             if step == 2:
                 spread(v_v, hold_v, P1V, 0)
-                spread(v_v, hold_v, P1V, 1)
-                spread(v_v, hold_v, P1V, NZ - 1)
+            if step >= 2:
+                spread(v_v, hold_v, P1V, step - 1)
+                spread(v_v, hold_v, P1V, NZ - step + 1)
     for dt in range(1, tp_size):
         remote(g_v, g_all.at[tp], GATHER, (me, lax.rem(tp + dt, tp_size)))
     local(g_v, g_all.at[tp], GATHER)
-    for dz in range(2, NZ - 1):
+    for dz in range(half - 1, half + 2):
         spread(v_v, hold_v, P1V, dz)
 
     loads[3].wait()

time: 96.1 us -> 98.2 us (1.022)
  the two profiles are of different devices: /device:TPU:64 before, /device:TPU:24 now
where the time goes in v5:
time: 98.2 us; the launch traced here: 98.1 us
  Pallas kernels  97.4 us (99%)
    pallas_call x1, Pallas kernels, shards(): pl.pallas_call(functools.partial(kernel, tp_size), out_shape=(out, out, n...  95.3 us
    pallas_call x1, Pallas kernels, shards(): pl.pallas_call(write_out, out_shape=(out, out, out), in_specs=[anywhere]...  2.13 us

profile of v5, /device:TPU:24, one launch (start us, length us, event | category | flops | bytes accessed | tf_op | source)
XLA Modules:
  0.0 98.1 jit_solution(924079626995119006)
XLA Ops:
  0.6 95.3 %shard_map.94 = (bf16[256,512]{1,0:T(8,128)(2,1)}, bf16[256,512]{1,0:T(8,128)(2,1)}, f32[4,256,128]{2,1,0:T(8,128)}, bf16[2,4,2,128,128]{4,3,2,1,0:T(8,128)(2,1)}) custom-call(s32[3,64]{1,0:T(4,128)} %bitcast.5, s32[64]{0:T(128)} %live.1, s32[3,64]{1,0:T(4,128)} %bitcast.6, bf16[256,512]{1,0:T(8,128)(2,1)} %g_hbm.1, bf16[512,4096]{1,0:T(8,128)(2,1)} %w_hbm.1, ...), custom_call_target="tpu_custom_call" | custom-call | tf_op jit(solution)/shard_map/pallas_call | solution.py:366
  95.9 2.1 %shard_map.95 = (bf16[256,512]{1,0:T(8,128)(2,1)}, bf16[256,512]{1,0:T(8,128)(2,1)}, bf16[256,512]{1,0:T(8,128)(2,1)}) custom-call(bf16[256,512]{1,0:T(8,128)(2,1)} %get-tuple-element.7.dq, bf16[256,512]{1,0:T(8,128)(2,1)} %get-tuple-element.8.dv, f32[4,256,128]{2,1,0:T(8,128)} %get-tuple-element.9.near_dk, bf16[2,4,2,128,128]{4,3,2,1,0:T(8,128)(2,1)} %get-tuple-element.10.fin_k), custom_call_target="tpu_custom_call" | custom-call | tf_op jit(solution)/shard_map/pallas_call | solution.py:402
